TPU v7x, 256 devices: a whole 4x4x8 slice. The times are simulated.
256 devices in a mesh: group: 8 (over z), tok: 32 (over y, x, core).
Axes of the slice: x: 4, y: 4, z: 8, core: 2. Of those that a mesh axis runs over, the one named last changes fastest.
Arguments:
- query_rows: bfloat16 [8, 8192, 256], P('group', 'tok'), may hold values from -6 to 6
- key_rows: bfloat16 [8, 8192, 256], P('group', 'tok'), may hold values from -6 to 6
- value_rows: bfloat16 [8, 8192, 256], P('group', 'tok'), may hold values from -6 to 6
- token_rates: bfloat16 [8, 8192], P('group', 'tok'), may hold values from 0.099609375 to 1
- gate_init: float32 [256, 256], P('tok'), may hold values from -0.375 to 0.375
- up_init: float32 [256, 256], P('tok'), may hold values from -0.375 to 0.375
- down_init: float32 [256, 256], P('tok'), may hold values from -0.375 to 0.375
Outputs:
- outputs: bfloat16 [8, 8192, 256], P('group', 'tok')
- gate_out: float32 [8, 256, 256], P('group', 'tok')
- up_out: float32 [8, 256, 256], P('group', 'tok')
- down_out: float32 [8, 256, 256], P('group', 'tok')
All inputs are finite; a program needn't handle non-finite values.
Results may differ from a plain program's by a relative error of at most 0.03.
Values may be sent and summed in bfloat16 or wider, within the bound.
A program may use at most 64 MiB of HBM per device.

v0:
```python
import jax
import jax.numpy as jnp
from jax import lax
from jax.sharding import PartitionSpec as P

NS_STEPS = 3


schulz_coeffs = (3.4445, -4.775, 2.0315)
update_scale = 0.5


def passed_along(array, axis, by):
    devices = lax.axis_size(axis)
    pairs = [(i, i + by) for i in range(devices) if 0 <= i + by < devices]
    return lax.ppermute(array, axis, pairs)


def silu_parts(pre_values):
    sigmoid_val = jax.nn.sigmoid(pre_values)
    return (pre_values * sigmoid_val, sigmoid_val * (1.0 + pre_values * (1.0 - sigmoid_val)))


def orthogonalize(gradient):
    scaled = gradient * lax.rsqrt(jnp.sum(gradient * gradient) + 1e-06)
    for repeat in range(NS_STEPS):
        gram_full = jnp.einsum("ik,jk->ij", scaled, scaled, precision=lax.Precision.HIGHEST)
        square = jnp.dot(gram_full, gram_full, precision=lax.Precision.HIGHEST)
        poly_full = schulz_coeffs[1] * gram_full + schulz_coeffs[2] * square
        scaled = schulz_coeffs[0] * scaled + jnp.dot(
            poly_full, scaled, precision=lax.Precision.HIGHEST
        )
    return scaled


def renormalize(stepped, before):
    target = jnp.sum(before * before, axis=0, keepdims=True)
    present = jnp.sum(stepped * stepped, axis=0, keepdims=True)
    return stepped * jnp.sqrt(target) * lax.rsqrt(present + 1e-06)


def advance(weights, key_block, value_block, rate_block):
    gate_low, up_low, down_low = [w.astype(jnp.bfloat16) for w in weights]
    gate_pre = jnp.dot(key_block, gate_low, preferred_element_type=jnp.float32)
    up_pre = jnp.dot(key_block, up_low, preferred_element_type=jnp.float32)
    act_full, slope = silu_parts(gate_pre)
    act_low = (act_full * up_pre).astype(jnp.bfloat16)
    out_grad = (
        -(rate_block[:, None].astype(jnp.float32) * value_block.astype(jnp.float32))
    ).astype(jnp.bfloat16)
    down_grad = jnp.einsum("th,td->hd", act_low, out_grad, preferred_element_type=jnp.float32)
    act_grad = jnp.einsum("td,hd->th", out_grad, down_low, preferred_element_type=jnp.float32)
    gate_diff = (act_grad * up_pre * slope).astype(jnp.bfloat16)
    up_diff = (act_grad * act_full).astype(jnp.bfloat16)
    gate_grad = jnp.einsum("td,th->dh", key_block, gate_diff, preferred_element_type=jnp.float32)
    up_grad = jnp.einsum("td,th->dh", key_block, up_diff, preferred_element_type=jnp.float32)
    grads = lax.psum((gate_grad, up_grad, down_grad), "tok")
    return tuple(
        (renormalize(w - update_scale * orthogonalize(g), w) for w, g in zip(weights, grads))
    )


def apply_fast(weights, query_block):
    gate_low, up_low, down_low = [w.astype(jnp.bfloat16) for w in weights]
    gate_pre = jnp.dot(query_block, gate_low, preferred_element_type=jnp.float32)
    up_pre = jnp.dot(query_block, up_low, preferred_element_type=jnp.float32)
    hidden = (jax.nn.silu(gate_pre) * up_pre).astype(jnp.bfloat16)
    return jnp.dot(hidden, down_low, preferred_element_type=jnp.float32).astype(jnp.bfloat16)


def flatten_all(weights):
    return jnp.concatenate([w.reshape(-1) for w in weights])


def unflatten_all(flat, shapes):
    pieces = []
    offset = 0
    for shape_pair in shapes:
        length = shape_pair[0] * shape_pair[1]
        pieces.append(flat[offset : offset + length].reshape(shape_pair))
        offset = offset + length
    return tuple(pieces)


def choose(flag, first, second):
    return tuple((jnp.where(flag, a_part, b_part) for a_part, b_part in zip(first, second)))


def body(query_rows, key_rows, value_rows, token_rates, gate_init, up_init, down_init):
    start = (
        lax.all_gather(gate_init, "tok", axis=0, tiled=True),
        lax.all_gather(up_init, "tok", axis=0, tiled=True),
        lax.all_gather(down_init, "tok", axis=0, tiled=True),
    )
    shapes = [w.shape for w in start]
    group_rank = lax.axis_index("group")
    group_total = lax.axis_size("group")
    current = start
    outgoing = start
    for section_idx in range(group_total):
        updated = advance(current, key_rows[0], value_rows[0], token_rates[0])
        outgoing = choose(group_rank == section_idx, updated, outgoing)
        if section_idx + 1 < group_total:
            passed = passed_along(flatten_all(updated), "group", 1)
            current = choose(group_rank == section_idx + 1, unflatten_all(passed, shapes), current)
    results = apply_fast(current, query_rows[0])[None]
    tok_rank = lax.axis_index("tok")
    tok_total = lax.axis_size("tok")
    sliced = []
    for weight in outgoing:
        row_share = weight.shape[0] // tok_total
        sliced.append(lax.dynamic_slice_in_dim(weight, tok_rank * row_share, row_share, 0)[None])
    return (results, sliced[0], sliced[1], sliced[2])


def solution(mesh):
    return jax.shard_map(
        body,
        mesh=mesh,
        in_specs=(
            P("group", "tok", None),
            P("group", "tok", None),
            P("group", "tok", None),
            P("group", "tok"),
            P("tok", None),
            P("tok", None),
            P("tok", None),
        ),
        out_specs=(
            P("group", "tok", None),
            P("group", "tok", None),
            P("group", "tok", None),
            P("group", "tok", None),
        ),
        check_vma=False,
    )
```

profile of v0, /device:TPU:1, one launch (start us, length us, event | category | flops | bytes accessed | tf_op | source)
XLA Modules:
  0.0 1406.7 jit_solution(6478373429651064685)
XLA Ops:
  7.9 26.5 %all_gather.9 = f32[256,256]{1,0:T(8,128)S(1)} all-gather(f32[8,256]{1,0:T(8,128)} %param.11), channel_id=1, replica_groups=mesh['group'=8,'tok'=32] {'tok'}, dimensions={0}, use_global_device_ids=true | all-gather | bytes 270336 | tf_op jit(solution)/shard_map/all_gather | solution.py:91
  34.5 24.1 %all_gather.11 = f32[256,256]{1,0:T(8,128)S(1)} all-gather(f32[8,256]{1,0:T(8,128)S(1)} %copy-done.68), channel_id=1, replica_groups=mesh['group'=8,'tok'=32] {'tok'}, dimensions={0}, use_global_device_ids=true | all-gather | bytes 270336 | tf_op jit(solution)/shard_map/all_gather | solution.py:92
  59.5 22.7 %all_gather.10 = f32[256,256]{1,0:T(8,128)S(1)} all-gather(f32[8,256]{1,0:T(8,128)S(1)} %copy-done.69), channel_id=1, replica_groups=mesh['group'=8,'tok'=32] {'tok'}, dimensions={0}, use_global_device_ids=true | all-gather | bytes 270336 | tf_op jit(solution)/shard_map/all_gather | solution.py:93
  83.4 1.0 convolution_bitcast_fusion.31
  86.3 113.8 %all-reduce.31.cloned.1.call-done = (f32[256,256]{0,1:T(8,128)}, f32[256,256]{0,1:T(8,128)}, f32[256,256]{0,1:T(8,128)}) async-done(((f32[256,256]{0,1:T(8,128)}, f32[256,256]{0,1:T(8,128)}, f32[256,256]{0,1:T(8,128)}), (f32[256,256]{0,1:T(8,128)}, f32[256,256]{0,1:T(8,128)}, f32[256,256]{0,1:T(8,128)})) %all-reduce.31.cloned.1.call-update) | async-done | bytes 786448 | tf_op jit(solution)/shard_map/psum | solution.py:57
  200.1 1.7 multiply_reduce_fusion.71
  202.5 1.7 multiply_reduce_fusion.65
  218.7 1.1 fusion.411
  222.8 4.1 collective-permute-start
  226.9 15.4 %collective-permute-done = f32[196608]{0:T(1024)} collective-permute-done((f32[196608]{0:T(1024)}, f32[196608]{0:T(1024)}, u32[]{:S(2)}, u32[]{:S(2)}) %collective-permute-start) | collective-permute-done | bytes 786464 | tf_op jit(solution)/shard_map/ppermute | solution.py:16
  242.3 1.2 fusion.409
  246.2 1.0 convolution_bitcast_fusion.27
  248.3 117.5 %all-reduce.29.cloned.1.call-done = (f32[256,256]{0,1:T(8,128)}, f32[256,256]{0,1:T(8,128)}, f32[256,256]{0,1:T(8,128)}) async-done(((f32[256,256]{0,1:T(8,128)}, f32[256,256]{0,1:T(8,128)}, f32[256,256]{0,1:T(8,128)}), (f32[256,256]{0,1:T(8,128)}, f32[256,256]{0,1:T(8,128)}, f32[256,256]{0,1:T(8,128)})) %all-reduce.29.cloned.1.call-update) | async-done | bytes 786448 | tf_op jit(solution)/shard_map/psum | solution.py:57
  365.8 1.7 multiply_reduce_fusion.62
  389.5 3.2 collective-permute-start.1
  392.7 16.3 %collective-permute-done.1 = f32[196608]{0:T(1024)S(1)} collective-permute-done((f32[196608]{0:T(1024)}, f32[196608]{0:T(1024)S(1)}, u32[]{:S(2)}, u32[]{:S(2)}) %collective-permute-start.1) | collective-permute-done | bytes 786464 | tf_op jit(solution)/shard_map/ppermute | solution.py:16
  411.8 1.0 convolution_bitcast_fusion.23
  413.9 117.4 %all-reduce.27.cloned.1.call-done = (f32[256,256]{0,1:T(8,128)}, f32[256,256]{0,1:T(8,128)}, f32[256,256]{0,1:T(8,128)}) async-done(((f32[256,256]{0,1:T(8,128)}, f32[256,256]{0,1:T(8,128)}, f32[256,256]{0,1:T(8,128)}), (f32[256,256]{0,1:T(8,128)}, f32[256,256]{0,1:T(8,128)}, f32[256,256]{0,1:T(8,128)})) %all-reduce.27.cloned.1.call-update) | async-done | bytes 786448 | tf_op jit(solution)/shard_map/psum | solution.py:57
  531.3 1.7 multiply_reduce_fusion.53
  552.9 4.1 collective-permute-start.2
  557.0 15.4 %collective-permute-done.2 = f32[196608]{0:T(1024)} collective-permute-done((f32[196608]{0:T(1024)}, f32[196608]{0:T(1024)}, u32[]{:S(2)}, u32[]{:S(2)}) %collective-permute-start.2) | collective-permute-done | bytes 786464 | tf_op jit(solution)/shard_map/ppermute | solution.py:16
  572.3 1.2 fusion.407
  576.2 1.0 convolution_bitcast_fusion.19
  578.4 117.5 %all-reduce.25.cloned.1.call-done = (f32[256,256]{0,1:T(8,128)}, f32[256,256]{0,1:T(8,128)}, f32[256,256]{0,1:T(8,128)}) async-done(((f32[256,256]{0,1:T(8,128)}, f32[256,256]{0,1:T(8,128)}, f32[256,256]{0,1:T(8,128)}), (f32[256,256]{0,1:T(8,128)}, f32[256,256]{0,1:T(8,128)}, f32[256,256]{0,1:T(8,128)})) %all-reduce.25.cloned.1.call-update) | async-done | bytes 786448 | tf_op jit(solution)/shard_map/psum | solution.py:57
  695.9 1.7 multiply_reduce_fusion.44
  718.8 4.0 collective-permute-start.3
  722.8 15.4 %collective-permute-done.3 = f32[196608]{0:T(1024)} collective-permute-done((f32[196608]{0:T(1024)}, f32[196608]{0:T(1024)}, u32[]{:S(2)}, u32[]{:S(2)}) %collective-permute-start.3) | collective-permute-done | bytes 786464 | tf_op jit(solution)/shard_map/ppermute | solution.py:16
  738.2 1.9 fusion.406
  747.2 117.6 %all-reduce.23.cloned.1.call-done = (f32[256,256]{0,1:T(8,128)}, f32[256,256]{0,1:T(8,128)}, f32[256,256]{0,1:T(8,128)}) async-done(((f32[256,256]{0,1:T(8,128)}, f32[256,256]{0,1:T(8,128)}, f32[256,256]{0,1:T(8,128)}), (f32[256,256]{0,1:T(8,128)}, f32[256,256]{0,1:T(8,128)}, f32[256,256]{0,1:T(8,128)})) %all-reduce.23.cloned.1.call-update) | async-done | bytes 786448 | tf_op jit(solution)/shard_map/psum | solution.py:57
  864.7 1.7 multiply_reduce_fusion.35
  889.6 4.0 collective-permute-start.4
  893.6 15.4 %collective-permute-done.4 = f32[196608]{0:T(1024)} collective-permute-done((f32[196608]{0:T(1024)}, f32[196608]{0:T(1024)}, u32[]{:S(2)}, u32[]{:S(2)}) %collective-permute-start.4) | collective-permute-done | bytes 786464 | tf_op jit(solution)/shard_map/ppermute | solution.py:16
  909.1 1.9 fusion.405
  915.9 1.0 convolution_bitcast_fusion.11
  918.0 117.6 %all-reduce.21.cloned.1.call-done = (f32[256,256]{0,1:T(8,128)}, f32[256,256]{0,1:T(8,128)}, f32[256,256]{0,1:T(8,128)}) async-done(((f32[256,256]{0,1:T(8,128)}, f32[256,256]{0,1:T(8,128)}, f32[256,256]{0,1:T(8,128)}), (f32[256,256]{0,1:T(8,128)}, f32[256,256]{0,1:T(8,128)}, f32[256,256]{0,1:T(8,128)})) %all-reduce.21.cloned.1.call-update) | async-done | bytes 786448 | tf_op jit(solution)/shard_map/psum | solution.py:57
  1035.6 1.7 multiply_reduce_fusion.26
  1060.2 4.0 collective-permute-start.5
  1064.2 15.4 %collective-permute-done.5 = f32[196608]{0:T(1024)} collective-permute-done((f32[196608]{0:T(1024)}, f32[196608]{0:T(1024)}, u32[]{:S(2)}, u32[]{:S(2)}) %collective-permute-start.5) | collective-permute-done | bytes 786464 | tf_op jit(solution)/shard_map/ppermute | solution.py:16
  1079.6 1.9 fusion.404
  1087.8 117.6 %all-reduce.19.cloned.1.call-done = (f32[256,256]{0,1:T(8,128)}, f32[256,256]{0,1:T(8,128)}, f32[256,256]{0,1:T(8,128)}) async-done(((f32[256,256]{0,1:T(8,128)}, f32[256,256]{0,1:T(8,128)}, f32[256,256]{0,1:T(8,128)}), (f32[256,256]{0,1:T(8,128)}, f32[256,256]{0,1:T(8,128)}, f32[256,256]{0,1:T(8,128)})) %all-reduce.19.cloned.1.call-update) | async-done | bytes 786448 | tf_op jit(solution)/shard_map/psum | solution.py:57
  1205.4 1.7 multiply_reduce_fusion.17
  1230.0 4.0 collective-permute-start.6
  1234.1 15.4 %collective-permute-done.6 = f32[196608]{0:T(1024)} collective-permute-done((f32[196608]{0:T(1024)}, f32[196608]{0:T(1024)}, u32[]{:S(2)}, u32[]{:S(2)}) %collective-permute-start.6) | collective-permute-done | bytes 786464 | tf_op jit(solution)/shard_map/ppermute | solution.py:16
  1249.5 1.9 fusion.403
  1256.2 1.0 convolution_bitcast_fusion.1
  1259.4 1.0 fusion.122
  1260.4 115.5 %all-reduce.17.cloned.1.call-done = (f32[256,256]{0,1:T(8,128)}, f32[256,256]{0,1:T(8,128)}, f32[256,256]{0,1:T(8,128)}) async-done(((f32[256,256]{0,1:T(8,128)}, f32[256,256]{0,1:T(8,128)}, f32[256,256]{0,1:T(8,128)}), (f32[256,256]{0,1:T(8,128)}, f32[256,256]{0,1:T(8,128)}, f32[256,256]{0,1:T(8,128)})) %all-reduce.17.cloned.1.call-update) | async-done | bytes 786448 | tf_op jit(solution)/shard_map/psum | solution.py:57
  1375.9 1.7 multiply_reduce_fusion.2
  (623 shorter events, 195.2 us)
Async XLA Ops:
  7.2 51.4 %copy-start = (bf16[1,256,256]{2,1,0:T(8,128)(2,1)S(1)}, bf16[1,256,256]{2,1,0:T(8,128)(2,1)}, u32[]{:S(2)}) copy-start(bf16[1,256,256]{2,1,0:T(8,128)(2,1)} %param.8) | copy-start | bytes 393220
  7.2 192.9 %all-reduce.31.cloned.1.call-start = ((), (), s32[]{:S(2)}) async-start(), calls=%async_computation.7 | async-start | bytes 1572864 | tf_op jit(solution)/shard_map/psum | solution.py:57
  7.9 26.5 %copy-start.68 = (f32[8,256]{1,0:T(8,128)S(1)}, f32[8,256]{1,0:T(8,128)}, u32[]{:S(2)}) copy-start(f32[8,256]{1,0:T(8,128)} %param.12) | copy-start | bytes 24580
  59.5 22.7 %copy-start.1 = (bf16[1,256,256]{2,1,0:T(8,128)(2,1)S(1)}, bf16[1,256,256]{2,1,0:T(8,128)(2,1)}, u32[]{:S(2)}) copy-start(bf16[1,256,256]{2,1,0:T(8,128)(2,1)} %param.9) | copy-start | bytes 393220
  85.5 280.4 %all-reduce.29.cloned.1.call-start = ((), (), s32[]{:S(2)}) async-start(), calls=%async_computation.6 | async-start | bytes 1572864 | tf_op jit(solution)/shard_map/psum | solution.py:57
  200.1 2.4 copy-start.11
  202.5 3.1 copy-start.18
  222.8 19.5 %collective-permute-start = (f32[196608]{0:T(1024)}, f32[196608]{0:T(1024)}, u32[]{:S(2)}, u32[]{:S(2)}) collective-permute-start(f32[196608]{0:T(1024)} %pad_maximum_fusion), channel_id=1, source_target_pairs={{0,32},{32,64},{64,96},{96,128},{128,160},{160,192},{192,224},{1,3... | collective-permute-start | bytes 2359304 | tf_op jit(solution)/shard_map/ppermute | solution.py:16
  248.2 283.1 %all-reduce.27.cloned.1.call-start = ((), (), s32[]{:S(2)}) async-start(), calls=%async_computation.5 | async-start | bytes 1572864 | tf_op jit(solution)/shard_map/psum | solution.py:57
  365.8 2.4 copy-start.10
  365.8 3.7 copy-start.19
  389.5 19.5 %collective-permute-start.1 = (f32[196608]{0:T(1024)}, f32[196608]{0:T(1024)S(1)}, u32[]{:S(2)}, u32[]{:S(2)}) collective-permute-start(f32[196608]{0:T(1024)} %pad_maximum_fusion.1), channel_id=1, source_target_pairs={{0,32},{32,64},{64,96},{96,128},{128,160},{160,192},{192,224},{1,3... | collective-permute-start | bytes 2359304 | tf_op jit(solution)/shard_map/ppermute | solution.py:16
  413.8 282.1 %all-reduce.25.cloned.1.call-start = ((), (), s32[]{:S(2)}) async-start(), calls=%async_computation.4 | async-start | bytes 1572864 | tf_op jit(solution)/shard_map/psum | solution.py:57
  531.3 2.4 copy-start.12
  531.3 3.7 copy-start.20
  552.9 19.5 %collective-permute-start.2 = (f32[196608]{0:T(1024)}, f32[196608]{0:T(1024)}, u32[]{:S(2)}, u32[]{:S(2)}) collective-permute-start(f32[196608]{0:T(1024)} %pad_maximum_fusion.2), channel_id=1, source_target_pairs={{0,32},{32,64},{64,96},{96,128},{128,160},{160,192},{192,224},{1,3... | collective-permute-start | bytes 2359304 | tf_op jit(solution)/shard_map/ppermute | solution.py:16
  578.3 286.5 %all-reduce.23.cloned.1.call-start = ((), (), s32[]{:S(2)}) async-start(), calls=%async_computation.3 | async-start | bytes 1572864 | tf_op jit(solution)/shard_map/psum | solution.py:57
  695.9 2.4 copy-start.13
  695.9 3.7 copy-start.21
  716.8 1.0 copy-start.48
  718.8 19.5 %collective-permute-start.3 = (f32[196608]{0:T(1024)}, f32[196608]{0:T(1024)}, u32[]{:S(2)}, u32[]{:S(2)}) collective-permute-start(f32[196608]{0:T(1024)} %pad_maximum_fusion.3), channel_id=1, source_target_pairs={{0,32},{32,64},{64,96},{96,128},{128,160},{160,192},{192,224},{1,3... | collective-permute-start | bytes 2359304 | tf_op jit(solution)/shard_map/ppermute | solution.py:16
  743.0 1.0 copy-start.65
  747.1 288.5 %all-reduce.21.cloned.1.call-start = ((), (), s32[]{:S(2)}) async-start(), calls=%async_computation.2 | async-start | bytes 1572864 | tf_op jit(solution)/shard_map/psum | solution.py:57
  864.7 2.4 copy-start.14
  864.7 3.7 copy-start.22
  887.6 1.0 copy-start.49
  889.6 19.5 %collective-permute-start.4 = (f32[196608]{0:T(1024)}, f32[196608]{0:T(1024)}, u32[]{:S(2)}, u32[]{:S(2)}) collective-permute-start(f32[196608]{0:T(1024)} %pad_maximum_fusion.4), channel_id=1, source_target_pairs={{0,32},{32,64},{64,96},{96,128},{128,160},{160,192},{192,224},{1,3... | collective-permute-start | bytes 2359304 | tf_op jit(solution)/shard_map/ppermute | solution.py:16
  913.9 1.0 copy-start.66
  917.9 287.4 %all-reduce.19.cloned.1.call-start = ((), (), s32[]{:S(2)}) async-start(), calls=%async_computation.1 | async-start | bytes 1572864 | tf_op jit(solution)/shard_map/psum | solution.py:57
  1035.6 2.4 copy-start.15
  1035.6 3.7 copy-start.23
  1058.2 1.0 copy-start.50
  1060.2 19.5 %collective-permute-start.5 = (f32[196608]{0:T(1024)}, f32[196608]{0:T(1024)}, u32[]{:S(2)}, u32[]{:S(2)}) collective-permute-start(f32[196608]{0:T(1024)} %pad_maximum_fusion.5), channel_id=1, source_target_pairs={{0,32},{32,64},{64,96},{96,128},{128,160},{160,192},{192,224},{1,3... | collective-permute-start | bytes 2359304 | tf_op jit(solution)/shard_map/ppermute | solution.py:16
  1087.7 288.2 %all-reduce.17.cloned.1.call-start = ((), (), s32[]{:S(2)}) async-start(), calls=%async_computation | async-start | bytes 1572864 | tf_op jit(solution)/shard_map/psum | solution.py:57
  1205.4 2.4 copy-start.16
  1205.4 3.7 copy-start.24
  1228.0 1.0 copy-start.51
  1230.0 19.5 %collective-permute-start.6 = (f32[196608]{0:T(1024)}, f32[196608]{0:T(1024)}, u32[]{:S(2)}, u32[]{:S(2)}) collective-permute-start(f32[196608]{0:T(1024)} %pad_maximum_fusion.6), channel_id=1, source_target_pairs={{0,32},{32,64},{64,96},{96,128},{128,160},{160,192},{192,224},{1,3... | collective-permute-start | bytes 2359304 | tf_op jit(solution)/shard_map/ppermute | solution.py:16
  1375.9 2.4 copy-start.17
  1375.9 3.7 copy-start.25
  1384.8 1.1 copy-start.43
  1384.8 1.2 copy-start.59
  1390.9 1.0 copy-start.35
  1390.9 1.1 copy-start.41
  1390.9 1.2 copy-start.58
  1392.1 1.0 copy-start.3
  1397.2 1.1 copy-start.39
  1397.2 1.2 copy-start.57
  (37 other events, 32.9 us)
Sparse Core Ops, SparseCore 0:
  85.6 114.4 all-reduce.30
  248.3 117.4 all-reduce.28
  413.9 117.3 all-reduce.26
  578.4 117.4 all-reduce.24
  747.2 117.4 all-reduce.22
  918.1 117.4 all-reduce.20
  1087.8 117.4 all-reduce.18
  1258.4 117.4 all-reduce.16
where the time goes:
time: 1410 us
  waiting for transfers between devices  1040 us (74%)
  matrix products  140 us (10%)
  blocking collectives  73.3 us (5%)
  local copies, waits for them, and re-layouts  46.4 us (3%)
  other arithmetic  41 us (3%)
  between operations  34.3 us (2%)
  starting transfers between devices  28.1 us (2%)
    psum x8, waiting for transfers between devices, advance(): grads = lax.psum((gate_grad, up_grad, down_grad), 'tok')  934 us
    ppermute x7, waiting for transfers between devices, passed_along(): return lax.ppermute(array, axis, pairs)  109 us
    dot_general x72, matrix products, orthogonalize(): jnp.einsum('ik,jk->ij', scaled, scaled, precision=lax.Precision.HIGHEST)  44.7 us
    dot_general x72, matrix products, orthogonalize(): jnp.dot(poly_full, scaled, precision=lax.Precision.HIGHEST)  32.3 us
  transfers between devices with their start and end apart: 15, of which 15 were waited for; matrix products, arithmetic and copies ran while one was open for 0% of the time, Pallas kernels for 0%

commit v1 on v0

v1 whole, which is shorter than its diff:
```python
import functools

import jax
import jax.numpy as jnp
from jax import lax
from jax.experimental import pallas as pl
from jax.experimental.pallas import tpu as pltpu
from jax.sharding import PartitionSpec as P

MESH = pl.DeviceIdType.MESH
NS_STEPS = 3
COEFF_A, COEFF_B, COEFF_C = (3.4445, -4.775, 2.0315)
UPDATE_SCALE = 0.5
f32, bf16 = jnp.float32, jnp.bfloat16
NN = (((1,), (0,)), ((), ()))
NT = (((1,), (1,)), ((), ()))


def dot(a, b, dims=NN):
    return lax.dot_general(a, b, dims, preferred_element_type=f32)


def split(a):
    high = a.astype(bf16)
    return high, (a - high.astype(f32)).astype(bf16)


def orthogonalize(grads):
    states = [g * lax.rsqrt(jnp.sum(g * g) + 1e-06) for g in grads]
    for _ in range(NS_STEPS):
        parts = [split(x) for x in states]
        grams = [dot(h, h, NT) for h, _ in parts]
        lows = [m.astype(bf16) for m in grams]
        squares = [dot(m, m) for m in lows]
        polys = [split(COEFF_B * m + COEFF_C * s) for m, s in zip(grams, squares)]
        states = [
            COEFF_A * x + (dot(nh, h) + (dot(nh, l) + dot(nl, h)))
            for x, (nh, nl), (h, l) in zip(states, polys, parts)
        ]
    return states


def kernel(
    groups, rows_y, rows_x,
    q_ref, k_ref, v_ref, r_ref, gi_ref, ui_ref, di_ref,
    oq_ref, og_ref, ou_ref, od_ref,
    ke, kbuf, sbuf, rbuf, gbuf, wg, state, wlow, osl, win, oin,
    feed_s, feed_r, rs_s, rs_r, ag_s, ag_r, fw_s, fw_r, in_s, in_r, if_s, if_r, w_s, w_r, o_s, o_r,
):
    chips = rows_y * rows_x
    g = lax.axis_index("group")
    tok = lax.axis_index("tok")
    core = lax.rem(tok, 2)
    chip = tok // 2
    py, px = chip // rows_x, lax.rem(chip, rows_x)
    sib = chip * 2 + (1 - core)
    tokens, width = ke.shape[1], ke.shape[2]
    hid = state.shape[1]
    half = hid // 2
    per = width * half // 128 // chips
    share = wg.shape[2]

    def ring(d, n):
        return min(d, n - d)

    offsets = [(dy, dx) for dy in range(rows_y) for dx in range(rows_x) if (dy, dx) != (0, 0)]
    offsets.sort(key=lambda o: -(ring(o[0], rows_y) + ring(o[1], rows_x)))
    count = len(offsets)

    def ahead(n):
        dy, dx = offsets[n]
        return lax.rem(py + dy, rows_y) * rows_x + lax.rem(px + dx, rows_x)

    def behind(n):
        dy, dx = offsets[n]
        return lax.rem(py + (rows_y - dy), rows_y) * rows_x + lax.rem(px + (rows_x - dx), rows_x)

    def copy(src, dst, send, recv, where):
        return pltpu.make_async_remote_copy(
            src_ref=src, dst_ref=dst, send_sem=send, recv_sem=recv, device_id=where, device_id_type=MESH
        )

    rate = jnp.broadcast_to(r_ref[...].astype(f32), (width, tokens)).T
    ke[0] = k_ref[0]
    ke[1] = (-(rate * v_ref[0].astype(f32))).astype(bf16)

    barrier = pltpu.get_barrier_semaphore()

    def query(weights):
        pre = dot(q_ref[0], weights[0], NT)
        up = dot(q_ref[0], weights[1], NT)
        hidden = (pre * (0.5 + 0.5 * jnp.tanh(0.5 * pre)) * up).astype(bf16)
        oq_ref[0] = dot(hidden, weights[2]).astype(bf16)

    def feed_copy(to):
        return copy(ke, kbuf.at[g, core], feed_s.at[to], feed_r.at[g, core], (0, chip * 2 + to))

    @pl.when(g > 0)
    def _():
        for to in range(2):
            pl.semaphore_signal(barrier, inc=1, device_id=(0, chip * 2 + to), device_id_type=MESH)
        pl.semaphore_wait(barrier, 2)
        feeds = [feed_copy(to) for to in range(2)]
        for f in feeds:
            f.start()
        copy(wlow, win, w_s, w_r, (0, tok)).wait_recv()
        query([win[m] for m in range(3)])
        copy(osl, oin, o_s, o_r, (0, tok)).wait_recv()
        og_ref[0] = oin[0]
        ou_ref[0] = oin[1]
        od_ref[0] = oin[2]
        for f in feeds:
            f.wait_send()

    @pl.when(g == 0)
    def _():
        kbuf[0, core] = ke[...]
        wg[tok, 0] = gi_ref[...]
        wg[tok, 1] = ui_ref[...]
        wg[tok, 2] = di_ref[...]
        for n in range(count):
            pl.semaphore_signal(barrier, inc=1, device_id=(0, ahead(n) * 2 + core), device_id_type=MESH)
        pl.semaphore_signal(barrier, inc=1, device_id=(0, sib), device_id_type=MESH)
        for z in range(1, groups):
            for to in range(2):
                pl.semaphore_signal(barrier, inc=1, device_id=(z, chip * 2 + to), device_id_type=MESH)
        pl.semaphore_wait(barrier, count + 1 + 2 * (groups - 1))

        def first_copy(n):
            return copy(wg.at[tok], wg.at[tok], in_s.at[n], in_r.at[n], (0, ahead(n) * 2 + core))

        def first_pass(n):
            slot = tok if n == count else behind(n) * 2 + core
            return copy(wg.at[slot], wg.at[slot], if_s.at[n], if_r.at[n], (0, sib))

        for n in range(count):
            first_copy(n).start()
        first_pass(count).start()
        feed = copy(ke, kbuf.at[0, core], feed_s.at[0], feed_r.at[0, core], (0, sib))
        feed.start()
        for n in reversed(range(count)):
            first_copy(n).wait_recv()
            first_pass(n).start()
        for n in reversed(range(count + 1)):
            first_pass(n).wait_recv()
        state[0] = wg[:, 0].reshape(width, hid).T
        state[1] = wg[:, 1].reshape(width, hid).T
        state[2] = wg[:, 2].reshape(hid, width)
        wlow[...] = state[...].astype(bf16)
        for n in range(count):
            first_copy(n).wait_send()
        for n in range(count + 1):
            first_pass(n).wait_send()
        feed.wait_send()

        def pick_outgoing():
            rows = lax.broadcasted_iota(jnp.int32, (16, width), 0)
            lanes = lax.broadcasted_iota(jnp.int32, (16, width), 1)
            for part in range(0, share, 16):
                size = min(16, share - part)
                one = jnp.where(lanes == rows + (tok * share + part), 1.0, 0.0).astype(bf16)
                for m in range(2):
                    full = state[m]
                    high, rest = split(full)
                    mid, low = split(full - high.astype(f32))
                    picked = dot(one, high, NT) + (dot(one, mid, NT) + dot(one, low, NT))
                    osl[m, part : part + size, :] = picked[:size]
            osl[2] = state[2, pl.ds(pl.multiple_of(tok * share, share), share), :]

        def slice_copy(n):
            return copy(
                sbuf.at[ahead(n)], rbuf.at[n], rs_s.at[n], rs_r.at[n], (0, ahead(n) * 2 + core)
            )

        def step(i, carry):
            par = lax.rem(i, 2)
            copy(ke, kbuf.at[i, 1 - core], feed_s.at[0], feed_r.at[i, 1 - core], (0, sib)).wait_recv()

            @pl.when(i > 0)
            def _():
                copy(ke, kbuf.at[i, core], feed_s.at[0], feed_r.at[i, core], (0, sib)).wait_recv()

            keys = kbuf[i, :, 0].reshape(2 * tokens, width)
            errs = kbuf[i, :, 1].reshape(2 * tokens, width)
            mine = pl.ds(pl.multiple_of(core * half, half), half)
            pre = dot(wlow[0, mine, :], keys, NT)
            up = dot(wlow[1, mine, :], keys, NT)
            back = dot(wlow[2, mine, :], errs, NT)
            sig = 0.5 + 0.5 * jnp.tanh(0.5 * pre)
            act = pre * sig
            slope = sig + act * (1.0 - sig)
            act_low = (act * up).astype(bf16)
            gate_diff = (back * up * slope).astype(bf16)
            up_diff = (back * act).astype(bf16)
            partial = (dot(gate_diff, keys), dot(up_diff, keys), dot(act_low, errs))
            for m in range(3):
                low = partial[m].astype(bf16)
                for s in range(width // 128):
                    span = chips * 128 // width
                    sbuf[s * span : (s + 1) * span, m] = low[:, s * 128 : (s + 1) * 128].reshape(
                        span, per, 128
                    )
            for n in range(count):
                slice_copy(n).start()

            weights_out = copy(wlow, win, w_s, w_r, (i, tok))
            slices_out = copy(osl, oin, o_s, o_r, (i - 1, tok))

            @pl.when(i == 0)
            def _():
                query([wlow[m] for m in range(3)])

            @pl.when(i > 0)
            def _():
                weights_out.start()
                pick_outgoing()

            @pl.when(i == 1)
            def _():
                og_ref[0] = osl[0]
                ou_ref[0] = osl[1]
                od_ref[0] = osl[2]

            @pl.when(i > 1)
            def _():
                slices_out.start()

            for n in reversed(range(count)):
                slice_copy(n).wait_recv()
            total = sbuf[chip].astype(f32)
            for n in range(count):
                total = total + rbuf[n].astype(f32)
            gbuf[par, core, chip] = total.astype(bf16)

            def sum_copy(n):
                slot = gbuf.at[par, core, chip]
                return copy(slot, slot, ag_s.at[n], ag_r.at[n], (0, ahead(n) * 2 + core))

            def pass_copy(n):
                slot = gbuf.at[par, core, chip if n == count else behind(n)]
                return copy(slot, slot, fw_s.at[n], fw_r.at[par, n], (0, sib))

            for n in range(count):
                sum_copy(n).start()
            pass_copy(count).start()
            for n in reversed(range(count)):
                sum_copy(n).wait_recv()
                pass_copy(n).start()
            for n in reversed(range(count + 1)):
                pass_copy(n).wait_recv()

            grads = []
            for m in range(3):
                sides = []
                for c in range(2):
                    span = chips * 128 // width
                    sides.append(
                        jnp.concatenate(
                            [
                                gbuf[par, c, s * span : (s + 1) * span, m].reshape(half, 128)
                                for s in range(width // 128)
                            ],
                            axis=1,
                        )
                    )
                grads.append(jnp.concatenate(sides, axis=0).astype(f32))
            ortho = orthogonalize(grads)

            for n in range(count):
                slice_copy(n).wait_send()
                sum_copy(n).wait_send()
            for n in range(count + 1):
                pass_copy(n).wait_send()

            @pl.when(i > 0)
            def _():
                weights_out.wait_send()

            @pl.when(i > 1)
            def _():
                slices_out.wait_send()

            for m in range(3):
                before = state[m]
                stepped = before - UPDATE_SCALE * ortho[m]
                axis = 0 if m == 2 else 1
                target = jnp.sum(before * before, axis=axis, keepdims=True)
                present = jnp.sum(stepped * stepped, axis=axis, keepdims=True)
                after = stepped * (jnp.sqrt(target) * lax.rsqrt(present + 1e-06))
                state[m] = after
                wlow[m] = after.astype(bf16)
            return carry

        lax.fori_loop(0, groups, step, 0)
        pick_outgoing()
        last = copy(osl, oin, o_s, o_r, (groups - 1, tok))
        last.start()
        last.wait_send()


def solution(mesh):
    groups, devices = mesh.shape["group"], mesh.shape["tok"]
    chips = devices // 2
    rows_y = 4 if chips == 16 else 2
    rows_x = chips // rows_y

    def body(query_rows, key_rows, value_rows, token_rates, gate_init, up_init, down_init):
        tokens, width = key_rows.shape[1:]
        share, hid = gate_init.shape
        share_w = down_init.shape[0]
        per = width * (hid // 2) // 128 // chips
        count = chips - 1
        vmem = pl.BlockSpec(memory_space=pltpu.VMEM)
        dma = pltpu.SemaphoreType.DMA
        return pl.pallas_call(
            functools.partial(kernel, groups, rows_y, rows_x),
            out_shape=(
                jax.ShapeDtypeStruct((1, tokens, width), bf16),
                jax.ShapeDtypeStruct((1, share, hid), f32),
                jax.ShapeDtypeStruct((1, share, hid), f32),
                jax.ShapeDtypeStruct((1, share_w, width), f32),
            ),
            in_specs=[vmem] * 7,
            out_specs=(vmem,) * 4,
            scratch_shapes=[
                pltpu.VMEM((2, tokens, width), bf16),
                pltpu.VMEM((groups, 2, 2, tokens, width), bf16),
                pltpu.VMEM((chips, 3, per, 128), bf16),
                pltpu.VMEM((count, 3, per, 128), bf16),
                pltpu.VMEM((2, 2, chips, 3, per, 128), bf16),
                pltpu.VMEM((devices, 3, share, hid), f32),
                pltpu.VMEM((3, hid, width), f32),
                pltpu.VMEM((3, hid, width), bf16),
                pltpu.VMEM((3, share, hid), f32),
                pltpu.VMEM((3, hid, width), bf16),
                pltpu.VMEM((3, share, hid), f32),
                dma((2,)),
                dma((groups, 2)),
                dma((count,)),
                dma((count,)),
                dma((count,)),
                dma((count,)),
                dma((chips,)),
                dma((2, chips)),
                dma((count,)),
                dma((count,)),
                dma((chips,)),
                dma((chips,)),
                dma,
                dma,
                dma,
                dma,
            ],
            compiler_params=pltpu.CompilerParams(
                collective_id=0, has_side_effects=True, vmem_limit_bytes=48 * 1024 * 1024
            ),
            cost_estimate=pl.CostEstimate(flops=10**10, bytes_accessed=10**7, transcendentals=10**6),
        )(query_rows, key_rows, value_rows, token_rates, gate_init, up_init, down_init)

    rows = P("group", "tok", None)
    return jax.shard_map(
        body,
        mesh=mesh,
        in_specs=(rows, rows, rows, P("group", "tok"), P("tok", None), P("tok", None), P("tok", None)),
        out_specs=(rows, rows, rows, rows),
        check_vma=False,
    )
```

time: 1410 us -> 155 us (0.11)
  waiting for transfers between devices: 1040 us -> 0 us
  Pallas kernels: 0 us -> 146 us
  matrix products: 140 us -> 0 us
  blocking collectives: 73.3 us -> 0 us
  other arithmetic: 41 us -> 0 us
  local copies, waits for them, and re-layouts: 46.4 us -> 7.92 us
  between operations: 34.3 us -> 0.66 us
  starting transfers between devices: 28.1 us -> 0 us
    psum x8 -> x0, waiting for transfers between devices: 934 us -> none  [advance(): grads = lax.psum((gate_grad, up_grad, down_grad), 'tok')]
    pallas_call x0 -> x1, Pallas kernels: none -> 146 us  [body(): pl.pallas_call(functools.partial(kernel, groups, rows_y, rows_x), out_sha...]
    dot_general x266 -> x0, matrix products: 140 us -> none  [the longest x72 44.7 us: orthogonalize(): jnp.einsum('ik,jk->ij', scaled, scaled, precision=lax.Precision.HIGHEST)]
    ppermute x7 -> x0, waiting for transfers between devices: 109 us -> none  [passed_along(): return lax.ppermute(array, axis, pairs)]
    all_gather x3 -> x0, blocking collectives: 73.3 us -> none  [the longest x1 26.5 us: body(): lax.all_gather(gate_init, 'tok', axis=0, tiled=True)]
    ppermute x7 -> x0, starting transfers between devices: 27.6 us -> none  [passed_along(): return lax.ppermute(array, axis, pairs)]
    reduce_sum x47 -> x0, other arithmetic: 27 us -> none  [the longest x23 24.4 us: orthogonalize(): scaled = gradient * lax.rsqrt(jnp.sum(gradient * gradient) + 1e-06)]
    unnamed x161 -> x18, local copies, waits for them, and re-layouts: 27.1 us -> 7.92 us
  transfers between devices with their start and end apart: 15 -> 0, of which waited for: 15 -> 0; matrix products, arithmetic and copies ran while one was open for 0% -> 0% of each run, Pallas kernels for 0% -> 0%
where the time goes in v1:
time: 155 us
  Pallas kernels  146 us (94%)
  local copies, waits for them, and re-layouts  7.92 us (5%)
    pallas_call x1, Pallas kernels, body(): pl.pallas_call(functools.partial(kernel, groups, rows_y, rows_x), out_sha...  146 us
    unnamed x18, local copies, waits for them, and re-layouts  7.92 us

profile of v1, /device:TPU:1, one launch (start us, length us, event | category | flops | bytes accessed | tf_op | source)
XLA Modules:
  0.0 154.9 jit_solution(10490956168719795872)
XLA Ops:
  0.6 0.0 copy-start
  0.6 0.9 copy-done
  1.5 0.0 copy-start.1
  1.5 0.9 copy-done.1
  2.4 0.0 copy-start.2
  2.4 0.9 copy-done.2
  3.3 0.0 copy-start.3
  3.4 0.7 copy-done.3
  4.0 0.0 copy-start.4
  4.0 0.7 copy-done.4
  4.7 0.0 copy-start.5
  4.7 0.7 copy-done.5
  5.4 0.0 copy-start.6
  5.4 0.7 copy-done.6
  6.1 146.3 %shard_map.102 = (bf16[1,256,256]{2,1,0:T(8,128)(2,1)S(1)}, f32[1,8,256]{2,1,0:T(8,128)S(1)}, f32[1,8,256]{2,1,0:T(8,128)S(1)}, f32[1,8,256]{2,1,0:T(8,128)S(1)}) custom-call(bf16[1,256,256]{2,1,0:T(8,128)(2,1)S(1)} %copy-done, bf16[1,256,256]{2,1,0:T(8,128)(2,1)S(1)} %copy-done.1, bf16[1,256,256]{2,1,0:T(8,128)(2,1)S(1)} %copy-done.2, ...), custom_call_target="tpu_custom_call" | custom-call | flops 10000000000 | bytes 10000000 | tf_op jit(solution)/shard_map/pallas_call | solution.py:315
  152.4 0.7 copy.15
  153.1 0.6 copy.16
  153.7 0.6 copy.17
  154.3 0.6 copy.18
Async XLA Ops:
  0.6 0.9 copy-start
  1.5 0.9 copy-start.1
  2.4 0.9 copy-start.2
  3.3 0.7 copy-start.3
  4.0 0.7 copy-start.4
  4.7 0.7 copy-start.5
  5.4 0.7 copy-start.6

commit v2 on v1

--- a/solution.py
+++ b/solution.py
@@ -44,8 +44,8 @@
     groups, rows_y, rows_x,
     q_ref, k_ref, v_ref, r_ref, gi_ref, ui_ref, di_ref,
     oq_ref, og_ref, ou_ref, od_ref,
-    ke, kbuf, sbuf, rbuf, gbuf, wg, state, wlow, osl, win, oin,
-    feed_s, feed_r, rs_s, rs_r, ag_s, ag_r, fw_s, fw_r, in_s, in_r, if_s, if_r, w_s, w_r, o_s, o_r,
+    qbuf, vbuf, rates, ke, kbuf, sbuf, rbuf, gbuf, wg, state, wlow, osl, win, oin,
+    load, feed_s, feed_r, rs_s, rs_r, ag_s, ag_r, fw_s, fw_r, in_s, in_r, if_s, if_r, w_s, w_r, o_s, o_r,
 ):
     chips = rows_y * rows_x
     g = lax.axis_index("group")
@@ -80,51 +80,62 @@
             src_ref=src, dst_ref=dst, send_sem=send, recv_sem=recv, device_id=where, device_id_type=MESH
         )
 
-    rate = jnp.broadcast_to(r_ref[...].astype(f32), (width, tokens)).T
-    ke[0] = k_ref[0]
-    ke[1] = (-(rate * v_ref[0].astype(f32))).astype(bf16)
-
+    loads = [
+        pltpu.make_async_copy(v_ref.at[0], vbuf, load.at[0]),
+        pltpu.make_async_copy(r_ref, rates, load.at[1]),
+        pltpu.make_async_copy(k_ref.at[0], ke.at[0], load.at[2]),
+        pltpu.make_async_copy(q_ref.at[0], qbuf, load.at[3]),
+    ]
     barrier = pltpu.get_barrier_semaphore()
 
+    def scale_values():
+        for n in range(3):
+            loads[n].wait()
+        rate = jnp.broadcast_to(rates[...].astype(f32), (width, tokens)).T
+        ke[1] = (-(rate * vbuf[...].astype(f32))).astype(bf16)
+
     def query(weights):
-        pre = dot(q_ref[0], weights[0], NT)
-        up = dot(q_ref[0], weights[1], NT)
+        pre = dot(qbuf[...], weights[0], NT)
+        up = dot(qbuf[...], weights[1], NT)
         hidden = (pre * (0.5 + 0.5 * jnp.tanh(0.5 * pre)) * up).astype(bf16)
         oq_ref[0] = dot(hidden, weights[2]).astype(bf16)
 
-    def feed_copy(to):
-        return copy(ke, kbuf.at[g, core], feed_s.at[to], feed_r.at[g, core], (0, chip * 2 + to))
-
     @pl.when(g > 0)
     def _():
-        for to in range(2):
-            pl.semaphore_signal(barrier, inc=1, device_id=(0, chip * 2 + to), device_id_type=MESH)
-        pl.semaphore_wait(barrier, 2)
-        feeds = [feed_copy(to) for to in range(2)]
-        for f in feeds:
-            f.start()
+        pl.semaphore_signal(barrier, inc=1, device_id=(0, tok), device_id_type=MESH)
+        for n in range(4):
+            loads[n].start()
+        scale_values()
+        pl.semaphore_wait(barrier, 1)
+        feed = copy(ke, kbuf.at[g, core], feed_s, feed_r.at[g, core], (0, tok))
+        feed.start()
+        loads[3].wait()
         copy(wlow, win, w_s, w_r, (0, tok)).wait_recv()
         query([win[m] for m in range(3)])
         copy(osl, oin, o_s, o_r, (0, tok)).wait_recv()
         og_ref[0] = oin[0]
         ou_ref[0] = oin[1]
         od_ref[0] = oin[2]
-        for f in feeds:
-            f.wait_send()
+        feed.wait_send()
 
     @pl.when(g == 0)
     def _():
-        kbuf[0, core] = ke[...]
-        wg[tok, 0] = gi_ref[...]
-        wg[tok, 1] = ui_ref[...]
-        wg[tok, 2] = di_ref[...]
+        firsts = [
+            pltpu.make_async_copy(ref, wg.at[tok, m], load.at[4 + m])
+            for m, ref in enumerate((gi_ref, ui_ref, di_ref))
+        ]
+        for c in firsts:
+            c.start()
+        for n in range(4):
+            loads[n].start()
         for n in range(count):
             pl.semaphore_signal(barrier, inc=1, device_id=(0, ahead(n) * 2 + core), device_id_type=MESH)
         pl.semaphore_signal(barrier, inc=1, device_id=(0, sib), device_id_type=MESH)
         for z in range(1, groups):
-            for to in range(2):
-                pl.semaphore_signal(barrier, inc=1, device_id=(z, chip * 2 + to), device_id_type=MESH)
-        pl.semaphore_wait(barrier, count + 1 + 2 * (groups - 1))
+            pl.semaphore_signal(barrier, inc=1, device_id=(z, tok), device_id_type=MESH)
+        for c in firsts:
+            c.wait()
+        pl.semaphore_wait(barrier, count + groups)
 
         def first_copy(n):
             return copy(wg.at[tok], wg.at[tok], in_s.at[n], in_r.at[n], (0, ahead(n) * 2 + core))
@@ -136,8 +147,11 @@
         for n in range(count):
             first_copy(n).start()
         first_pass(count).start()
-        feed = copy(ke, kbuf.at[0, core], feed_s.at[0], feed_r.at[0, core], (0, sib))
+        scale_values()
+        kbuf[0, core] = ke[...]
+        feed = copy(ke, kbuf.at[0, core], feed_s, feed_r.at[0, core], (0, sib))
         feed.start()
+        loads[3].wait()
         for n in reversed(range(count)):
             first_copy(n).wait_recv()
             first_pass(n).start()
@@ -174,12 +188,7 @@
 
         def step(i, carry):
             par = lax.rem(i, 2)
-            copy(ke, kbuf.at[i, 1 - core], feed_s.at[0], feed_r.at[i, 1 - core], (0, sib)).wait_recv()
-
-            @pl.when(i > 0)
-            def _():
-                copy(ke, kbuf.at[i, core], feed_s.at[0], feed_r.at[i, core], (0, sib)).wait_recv()
-
+            copy(ke, kbuf.at[i, 1 - core], feed_s, feed_r.at[i, 1 - core], (0, sib)).wait_recv()
             keys = kbuf[i, :, 0].reshape(2 * tokens, width)
             errs = kbuf[i, :, 1].reshape(2 * tokens, width)
             mine = pl.ds(pl.multiple_of(core * half, half), half)
@@ -249,6 +258,16 @@
             for n in reversed(range(count + 1)):
                 pass_copy(n).wait_recv()
 
+            coming = jnp.minimum(i + 1, groups - 1)
+            pass_feed = copy(
+                kbuf.at[coming, core], kbuf.at[coming, core], feed_s, feed_r.at[coming, core], (0, sib)
+            )
+
+            @pl.when(i < groups - 1)
+            def _():
+                pass_feed.wait_recv()
+                pass_feed.start()
+
             grads = []
             for m in range(3):
                 sides = []
@@ -266,6 +285,10 @@
                 grads.append(jnp.concatenate(sides, axis=0).astype(f32))
             ortho = orthogonalize(grads)
 
+            @pl.when(i < groups - 1)
+            def _():
+                pass_feed.wait_send()
+
             for n in range(count):
                 slice_copy(n).wait_send()
                 sum_copy(n).wait_send()
@@ -320,9 +343,12 @@
                 jax.ShapeDtypeStruct((1, share, hid), f32),
                 jax.ShapeDtypeStruct((1, share_w, width), f32),
             ),
-            in_specs=[vmem] * 7,
+            in_specs=[pl.BlockSpec(memory_space=pltpu.MemorySpace.HBM)] * 7,
             out_specs=(vmem,) * 4,
             scratch_shapes=[
+                pltpu.VMEM((tokens, width), bf16),
+                pltpu.VMEM((tokens, width), bf16),
+                pltpu.VMEM((1, tokens), bf16),
                 pltpu.VMEM((2, tokens, width), bf16),
                 pltpu.VMEM((groups, 2, 2, tokens, width), bf16),
                 pltpu.VMEM((chips, 3, per, 128), bf16),
@@ -334,7 +360,8 @@
                 pltpu.VMEM((3, share, hid), f32),
                 pltpu.VMEM((3, hid, width), bf16),
                 pltpu.VMEM((3, share, hid), f32),
-                dma((2,)),
+                dma((7,)),
+                dma,
                 dma((groups, 2)),
                 dma((count,)),
                 dma((count,)),
@@ -352,7 +379,7 @@
                 dma,
             ],
             compiler_params=pltpu.CompilerParams(
-                collective_id=0, has_side_effects=True, vmem_limit_bytes=48 * 1024 * 1024
+                collective_id=0, has_side_effects=True, vmem_limit_bytes=63 * 1024 * 1024
             ),
             cost_estimate=pl.CostEstimate(flops=10**10, bytes_accessed=10**7, transcendentals=10**6),
         )(query_rows, key_rows, value_rows, token_rates, gate_init, up_init, down_init)

time: 155 us -> 148 us (0.955)
  local copies, waits for them, and re-layouts: 7.92 us -> 3.58 us
  Pallas kernels: 146 us -> 143 us
    unnamed x18 -> x10, local copies, waits for them, and re-layouts: 7.92 us -> 3.58 us
    pallas_call x1, Pallas kernels: 146 us -> 143 us  [body(): pl.pallas_call(functools.partial(kernel, groups, rows_y, rows_x), out_sha...]
where the time goes in v2:
time: 148 us; the launch traced here: 147 us
  Pallas kernels  143 us (97%)
  local copies, waits for them, and re-layouts  3.58 us (2%)
    pallas_call x1, Pallas kernels, body(): pl.pallas_call(functools.partial(kernel, groups, rows_y, rows_x), out_sha...  143 us
    unnamed x10, local copies, waits for them, and re-layouts  3.58 us

profile of v2, /device:TPU:1, one launch (start us, length us, event | category | flops | bytes accessed | tf_op | source)
XLA Modules:
  0.0 147.4 jit_solution(12447784202845047118)
XLA Ops:
  0.6 143.2 %shard_map.102 = (bf16[1,256,256]{2,1,0:T(8,128)(2,1)}, f32[1,8,256]{2,1,0:T(8,128)}, f32[1,8,256]{2,1,0:T(8,128)}, f32[1,8,256]{2,1,0:T(8,128)}) custom-call(bf16[1,256,256]{2,1,0:T(8,128)(2,1)} %q_ref.1, bf16[1,256,256]{2,1,0:T(8,128)(2,1)} %k_ref.1, bf16[1,256,256]{2,1,0:T(8,128)(2,1)} %v_ref.1, bf16[1,256]{1,0:T(2,128)(2,1)} %r_ref.1, f32[8,256]{1,0:T(8,128)} %gi_ref.1, ...), custom_call_target="tpu_custom_call" | custom-call | flops 10000000000 | bytes 10000000 | tf_op jit(solution)/shard_map/pallas_call | solution.py:338
  143.8 0.0 copy-start.2
  143.8 1.6 %copy.15 = bf16[1,256,256]{2,1,0:T(8,128)(2,1)} copy(bf16[1,256,256]{2,1,0:T(8,128)(2,1)} %get-tuple-element.8) | data formatting | bytes 262144
  145.4 0.0 copy-done.2
  145.4 0.0 copy-start.1
  145.4 0.6 copy.16
  146.0 0.1 copy-done.1
  146.1 0.0 copy-start
  146.1 0.6 copy.17
  146.7 0.1 copy-done
  146.8 0.6 copy.18
Async XLA Ops:
  143.8 1.6 %copy-start.2 = (f32[1,8,256]{2,1,0:T(8,128)S(1)}, f32[1,8,256]{2,1,0:T(8,128)}, u32[]{:S(2)}) copy-start(f32[1,8,256]{2,1,0:T(8,128)} %get-tuple-element.9) | copy-start | bytes 24580
  145.4 0.7 copy-start.1
  146.1 0.7 copy-start

commit v3 on v2

--- a/solution.py
+++ b/solution.py
@@ -27,16 +27,20 @@
 
 def orthogonalize(grads):
     states = [g * lax.rsqrt(jnp.sum(g * g) + 1e-06) for g in grads]
-    for _ in range(NS_STEPS):
-        parts = [split(x) for x in states]
-        grams = [dot(h, h, NT) for h, _ in parts]
+    for repeat in range(NS_STEPS):
+        highs = [x.astype(bf16) for x in states]
+        grams = [dot(h, h, NT) for h in highs]
         lows = [m.astype(bf16) for m in grams]
         squares = [dot(m, m) for m in lows]
-        polys = [split(COEFF_B * m + COEFF_C * s) for m, s in zip(grams, squares)]
-        states = [
-            COEFF_A * x + (dot(nh, h) + (dot(nh, l) + dot(nl, h)))
-            for x, (nh, nl), (h, l) in zip(states, polys, parts)
-        ]
+        polys = [COEFF_B * m + COEFF_C * s for m, s in zip(grams, squares)]
+        if repeat + 1 < NS_STEPS:
+            moves = [dot(p.astype(bf16), h) for p, h in zip(polys, highs)]
+        else:
+            moves = []
+            for p, x in zip(polys, states):
+                (ph, pl_), (xh, xl) = split(p), split(x)
+                moves.append(dot(ph, xh) + (dot(ph, xl) + dot(pl_, xh)))
+        states = [COEFF_A * x + m for x, m in zip(states, moves)]
     return states
 
 
@@ -185,6 +189,20 @@
             return copy(
                 sbuf.at[ahead(n)], rbuf.at[n], rs_s.at[n], rs_r.at[n], (0, ahead(n) * 2 + core)
             )
+
+        def sum_copy(par, n):
+            slot = gbuf.at[par, core, chip]
+            return copy(slot, slot, ag_s.at[n], ag_r.at[n], (0, ahead(n) * 2 + core))
+
+        def pass_copy(par, n):
+            slot = gbuf.at[par, core, chip if n == count else behind(n)]
+            return copy(slot, slot, fw_s.at[n], fw_r.at[par, n], (0, sib))
+
+        def sums_sent(par):
+            for n in range(count):
+                sum_copy(par, n).wait_send()
+            for n in range(count + 1):
+                pass_copy(par, n).wait_send()
 
         def step(i, carry):
             par = lax.rem(i, 2)
@@ -223,6 +241,7 @@
             def _():
                 weights_out.start()
                 pick_outgoing()
+                sums_sent(1 - par)
 
             @pl.when(i == 1)
             def _():
@@ -241,22 +260,16 @@
                 total = total + rbuf[n].astype(f32)
             gbuf[par, core, chip] = total.astype(bf16)
 
-            def sum_copy(n):
-                slot = gbuf.at[par, core, chip]
-                return copy(slot, slot, ag_s.at[n], ag_r.at[n], (0, ahead(n) * 2 + core))
-
-            def pass_copy(n):
-                slot = gbuf.at[par, core, chip if n == count else behind(n)]
-                return copy(slot, slot, fw_s.at[n], fw_r.at[par, n], (0, sib))
-
             for n in range(count):
-                sum_copy(n).start()
-            pass_copy(count).start()
+                sum_copy(par, n).start()
+            pass_copy(par, count).start()
+            for n in range(count):
+                slice_copy(n).wait_send()
             for n in reversed(range(count)):
-                sum_copy(n).wait_recv()
-                pass_copy(n).start()
+                sum_copy(par, n).wait_recv()
+                pass_copy(par, n).start()
             for n in reversed(range(count + 1)):
-                pass_copy(n).wait_recv()
+                pass_copy(par, n).wait_recv()
 
             coming = jnp.minimum(i + 1, groups - 1)
             pass_feed = copy(
@@ -289,12 +302,6 @@
             def _():
                 pass_feed.wait_send()
 
-            for n in range(count):
-                slice_copy(n).wait_send()
-                sum_copy(n).wait_send()
-            for n in range(count + 1):
-                pass_copy(n).wait_send()
-
             @pl.when(i > 0)
             def _():
                 weights_out.wait_send()
@@ -318,6 +325,7 @@
         pick_outgoing()
         last = copy(osl, oin, o_s, o_r, (groups - 1, tok))
         last.start()
+        sums_sent((groups - 1) % 2)
         last.wait_send()
 
 

time: 148 us -> 145 us (0.980)
  Pallas kernels: 143 us -> 140 us
    pallas_call x1, Pallas kernels: 143 us -> 140 us  [body(): pl.pallas_call(functools.partial(kernel, groups, rows_y, rows_x), out_sha...]
where the time goes in v3:
time: 145 us; the launch traced here: 144 us
  Pallas kernels  140 us (97%)
  local copies, waits for them, and re-layouts  3.58 us (2%)
    pallas_call x1, Pallas kernels, body(): pl.pallas_call(functools.partial(kernel, groups, rows_y, rows_x), out_sha...  140 us
    unnamed x10, local copies, waits for them, and re-layouts  3.58 us

profile of v3, /device:TPU:1, one launch (start us, length us, event | category | flops | bytes accessed | tf_op | source)
XLA Modules:
  0.0 144.5 jit_solution(13222629400940700034)
XLA Ops:
  0.6 140.2 %shard_map.102 = (bf16[1,256,256]{2,1,0:T(8,128)(2,1)}, f32[1,8,256]{2,1,0:T(8,128)}, f32[1,8,256]{2,1,0:T(8,128)}, f32[1,8,256]{2,1,0:T(8,128)}) custom-call(bf16[1,256,256]{2,1,0:T(8,128)(2,1)} %q_ref.1, bf16[1,256,256]{2,1,0:T(8,128)(2,1)} %k_ref.1, bf16[1,256,256]{2,1,0:T(8,128)(2,1)} %v_ref.1, bf16[1,256]{1,0:T(2,128)(2,1)} %r_ref.1, f32[8,256]{1,0:T(8,128)} %gi_ref.1, ...), custom_call_target="tpu_custom_call" | custom-call | flops 10000000000 | bytes 10000000 | tf_op jit(solution)/shard_map/pallas_call | solution.py:346
  140.9 0.0 copy-start.2
  140.9 1.6 %copy.15 = bf16[1,256,256]{2,1,0:T(8,128)(2,1)} copy(bf16[1,256,256]{2,1,0:T(8,128)(2,1)} %get-tuple-element.8) | data formatting | bytes 262144
  142.5 0.0 copy-done.2
  142.5 0.0 copy-start.1
  142.5 0.6 copy.16
  143.1 0.1 copy-done.1
  143.2 0.0 copy-start
  143.2 0.6 copy.17
  143.8 0.1 copy-done
  143.9 0.6 copy.18
Async XLA Ops:
  140.9 1.6 %copy-start.2 = (f32[1,8,256]{2,1,0:T(8,128)S(1)}, f32[1,8,256]{2,1,0:T(8,128)}, u32[]{:S(2)}) copy-start(f32[1,8,256]{2,1,0:T(8,128)} %get-tuple-element.9) | copy-start | bytes 24580
  142.5 0.7 copy-start.1
  143.2 0.7 copy-start

commit v4 on v3

--- a/solution.py
+++ b/solution.py
@@ -335,7 +335,8 @@
     rows_y = 4 if chips == 16 else 2
     rows_x = chips // rows_y
 
-    def body(query_rows, key_rows, value_rows, token_rates, gate_init, up_init, down_init):
+    def body(*args):
+        _, key_rows, _, _, gate_init, _, down_init = args
         tokens, width = key_rows.shape[1:]
         share, hid = gate_init.shape
         share_w = down_init.shape[0]
@@ -387,10 +388,10 @@
                 dma,
             ],
             compiler_params=pltpu.CompilerParams(
-                collective_id=0, has_side_effects=True, vmem_limit_bytes=63 * 1024 * 1024
+                collective_id=0, has_side_effects=True, vmem_limit_bytes=48 * 1024 * 1024
             ),
             cost_estimate=pl.CostEstimate(flops=10**10, bytes_accessed=10**7, transcendentals=10**6),
-        )(query_rows, key_rows, value_rows, token_rates, gate_init, up_init, down_init)
+        )(*[pltpu.with_memory_space_constraint(x, pltpu.MemorySpace.HBM) for x in args])
 
     rows = P("group", "tok", None)
     return jax.shard_map(

time: 145 us -> 142 us (0.979)
    unnamed x10 -> x4, local copies, waits for them, and re-layouts: 3.58 us -> 2.45 us
where the time goes in v4:
time: 142 us
  Pallas kernels  139 us (98%)
  local copies, waits for them, and re-layouts  2.45 us (2%)
    pallas_call x1, Pallas kernels, body(): pl.pallas_call(functools.partial(kernel, groups, rows_y, rows_x), out_sha...  139 us

profile of v4, /device:TPU:1, one launch (start us, length us, event | category | flops | bytes accessed | tf_op | source)
XLA Modules:
  0.0 142.2 jit_solution(6568390511553647876)
XLA Ops:
  0.6 139.1 %shard_map.102 = (bf16[1,256,256]{2,1,0:T(8,128)(2,1)S(1)}, f32[1,8,256]{2,1,0:T(8,128)S(1)}, f32[1,8,256]{2,1,0:T(8,128)S(1)}, f32[1,8,256]{2,1,0:T(8,128)S(1)}) custom-call(bf16[1,256,256]{2,1,0:T(8,128)(2,1)} %q_ref.1, bf16[1,256,256]{2,1,0:T(8,128)(2,1)} %k_ref.1, bf16[1,256,256]{2,1,0:T(8,128)(2,1)} %v_ref.1, bf16[1,256]{1,0:T(2,128)(2,1)} %r_ref.1, ...), custom_call_target="tpu_custom_call" | custom-call | flops 10000000000 | bytes 10000000 | tf_op jit(solution)/shard_map/pallas_call | solution.py:347
  139.8 0.7 copy.15
  140.4 0.6 copy.16
  141.0 0.6 copy.17
  141.6 0.6 copy.18

commit v5 on v4

--- a/solution.py
+++ b/solution.py
@@ -106,7 +106,6 @@
 
     @pl.when(g > 0)
     def _():
-        pl.semaphore_signal(barrier, inc=1, device_id=(0, tok), device_id_type=MESH)
         for n in range(4):
             loads[n].start()
         scale_values()
@@ -124,6 +123,8 @@
 
     @pl.when(g == 0)
     def _():
+        for z in range(1, groups):
+            pl.semaphore_signal(barrier, inc=1, device_id=(z, tok), device_id_type=MESH)
         firsts = [
             pltpu.make_async_copy(ref, wg.at[tok, m], load.at[4 + m])
             for m, ref in enumerate((gi_ref, ui_ref, di_ref))
@@ -135,11 +136,9 @@
         for n in range(count):
             pl.semaphore_signal(barrier, inc=1, device_id=(0, ahead(n) * 2 + core), device_id_type=MESH)
         pl.semaphore_signal(barrier, inc=1, device_id=(0, sib), device_id_type=MESH)
-        for z in range(1, groups):
-            pl.semaphore_signal(barrier, inc=1, device_id=(z, tok), device_id_type=MESH)
         for c in firsts:
             c.wait()
-        pl.semaphore_wait(barrier, count + groups)
+        pl.semaphore_wait(barrier, count + 1)
 
         def first_copy(n):
             return copy(wg.at[tok], wg.at[tok], in_s.at[n], in_r.at[n], (0, ahead(n) * 2 + core))

time: 142 us -> 139 us (0.979)
  Pallas kernels: 139 us -> 136 us
    pallas_call x1, Pallas kernels: 139 us -> 136 us  [body(): pl.pallas_call(functools.partial(kernel, groups, rows_y, rows_x), out_sha...]
where the time goes in v5:
time: 139 us
  Pallas kernels  136 us (98%)
  local copies, waits for them, and re-layouts  2.45 us (2%)
    pallas_call x1, Pallas kernels, body(): pl.pallas_call(functools.partial(kernel, groups, rows_y, rows_x), out_sha...  136 us

profile of v5, /device:TPU:1, one launch (start us, length us, event | category | flops | bytes accessed | tf_op | source)
XLA Modules:
  0.0 138.6 jit_solution(17379197149683587194)
XLA Ops:
  0.6 135.6 %shard_map.102 = (bf16[1,256,256]{2,1,0:T(8,128)(2,1)S(1)}, f32[1,8,256]{2,1,0:T(8,128)S(1)}, f32[1,8,256]{2,1,0:T(8,128)S(1)}, f32[1,8,256]{2,1,0:T(8,128)S(1)}) custom-call(bf16[1,256,256]{2,1,0:T(8,128)(2,1)} %q_ref.1, bf16[1,256,256]{2,1,0:T(8,128)(2,1)} %k_ref.1, bf16[1,256,256]{2,1,0:T(8,128)(2,1)} %v_ref.1, bf16[1,256]{1,0:T(2,128)(2,1)} %r_ref.1, ...), custom_call_target="tpu_custom_call" | custom-call | flops 10000000000 | bytes 10000000 | tf_op jit(solution)/shard_map/pallas_call | solution.py:346
  136.2 0.7 copy.15
  136.9 0.6 copy.16
  137.5 0.6 copy.17
  138.1 0.6 copy.18

commit v6 on v5

--- a/solution.py
+++ b/solution.py
@@ -26,28 +26,38 @@
 
 
 def orthogonalize(grads):
-    states = [g * lax.rsqrt(jnp.sum(g * g) + 1e-06) for g in grads]
+    wide = [g.astype(f32) for g in grads]
+    scales = [lax.rsqrt(jnp.sum(g * g) + 1e-06) for g in wide]
+    states = None
     for repeat in range(NS_STEPS):
-        highs = [x.astype(bf16) for x in states]
-        grams = [dot(h, h, NT) for h in highs]
+        if repeat == 0:
+            highs = grads
+            grams = [(s * s) * dot(h, h, NT) for h, s in zip(highs, scales)]
+        else:
+            highs = [x.astype(bf16) for x in states]
+            grams = [dot(h, h, NT) for h in highs]
         lows = [m.astype(bf16) for m in grams]
         squares = [dot(m, m) for m in lows]
         polys = [COEFF_B * m + COEFF_C * s for m, s in zip(grams, squares)]
-        if repeat + 1 < NS_STEPS:
+        if repeat == 0:
             moves = [dot(p.astype(bf16), h) for p, h in zip(polys, highs)]
+            states = [s * (COEFF_A * x + m) for s, x, m in zip(scales, wide, moves)]
+        elif repeat + 1 < NS_STEPS:
+            moves = [dot(p.astype(bf16), h) for p, h in zip(polys, highs)]
+            states = [COEFF_A * x + m for x, m in zip(states, moves)]
         else:
             moves = []
             for p, x in zip(polys, states):
                 (ph, pl_), (xh, xl) = split(p), split(x)
                 moves.append(dot(ph, xh) + (dot(ph, xl) + dot(pl_, xh)))
-        states = [COEFF_A * x + m for x, m in zip(states, moves)]
+            states = [COEFF_A * x + m for x, m in zip(states, moves)]
     return states
 
 
 def kernel(
     groups, rows_y, rows_x,
     q_ref, k_ref, v_ref, r_ref, gi_ref, ui_ref, di_ref,
-    oq_ref, og_ref, ou_ref, od_ref,
+    oq_ref, rows_ref,
     qbuf, vbuf, rates, ke, kbuf, sbuf, rbuf, gbuf, wg, state, wlow, osl, win, oin,
     load, feed_s, feed_r, rs_s, rs_r, ag_s, ag_r, fw_s, fw_r, in_s, in_r, if_s, if_r, w_s, w_r, o_s, o_r,
 ):
@@ -116,9 +126,7 @@
         copy(wlow, win, w_s, w_r, (0, tok)).wait_recv()
         query([win[m] for m in range(3)])
         copy(osl, oin, o_s, o_r, (0, tok)).wait_recv()
-        og_ref[0] = oin[0]
-        ou_ref[0] = oin[1]
-        od_ref[0] = oin[2]
+        rows_ref[...] = oin[...]
         feed.wait_send()
 
     @pl.when(g == 0)
@@ -244,9 +252,7 @@
 
             @pl.when(i == 1)
             def _():
-                og_ref[0] = osl[0]
-                ou_ref[0] = osl[1]
-                od_ref[0] = osl[2]
+                rows_ref[...] = osl[...]
 
             @pl.when(i > 1)
             def _():
@@ -294,7 +300,7 @@
                             axis=1,
                         )
                     )
-                grads.append(jnp.concatenate(sides, axis=0).astype(f32))
+                grads.append(jnp.concatenate(sides, axis=0))
             ortho = orthogonalize(grads)
 
             @pl.when(i < groups - 1)
@@ -343,16 +349,14 @@
         count = chips - 1
         vmem = pl.BlockSpec(memory_space=pltpu.VMEM)
         dma = pltpu.SemaphoreType.DMA
-        return pl.pallas_call(
+        outputs, slices = pl.pallas_call(
             functools.partial(kernel, groups, rows_y, rows_x),
             out_shape=(
                 jax.ShapeDtypeStruct((1, tokens, width), bf16),
-                jax.ShapeDtypeStruct((1, share, hid), f32),
-                jax.ShapeDtypeStruct((1, share, hid), f32),
-                jax.ShapeDtypeStruct((1, share_w, width), f32),
+                jax.ShapeDtypeStruct((3, share, hid), f32),
             ),
             in_specs=[pl.BlockSpec(memory_space=pltpu.MemorySpace.HBM)] * 7,
-            out_specs=(vmem,) * 4,
+            out_specs=(vmem,) * 2,
             scratch_shapes=[
                 pltpu.VMEM((tokens, width), bf16),
                 pltpu.VMEM((tokens, width), bf16),
@@ -391,6 +395,7 @@
             ),
             cost_estimate=pl.CostEstimate(flops=10**10, bytes_accessed=10**7, transcendentals=10**6),
         )(*[pltpu.with_memory_space_constraint(x, pltpu.MemorySpace.HBM) for x in args])
+        return outputs, slices[0:1], slices[1:2], slices[2:3]
 
     rows = P("group", "tok", None)
     return jax.shard_map(

time: 139 us -> 136 us (0.978)
  Pallas kernels: 136 us -> 134 us
    pallas_call x1, Pallas kernels: 136 us -> 134 us  [body(): pl.pallas_call(functools.partial(kernel, groups, rows_y, rows_x), out_sha...]
    unnamed x4 -> x1, local copies, waits for them, and re-layouts: 2.45 us -> 0.65 us
where the time goes in v6:
time: 136 us
  Pallas kernels  134 us (99%)
    pallas_call x1, Pallas kernels, body(): pl.pallas_call(functools.partial(kernel, groups, rows_y, rows_x), out_sha...  134 us

profile of v6, /device:TPU:1, one launch (start us, length us, event | category | flops | bytes accessed | tf_op | source)
XLA Modules:
  0.0 135.6 jit_solution(9969643359245029814)
XLA Ops:
  0.6 133.7 %shard_map.102 = (bf16[1,256,256]{2,1,0:T(8,128)(2,1)S(1)}, f32[3,8,256]{2,1,0:T(8,128)S(1)}) custom-call(bf16[1,256,256]{2,1,0:T(8,128)(2,1)} %q_ref.1, bf16[1,256,256]{2,1,0:T(8,128)(2,1)} %k_ref.1, bf16[1,256,256]{2,1,0:T(8,128)(2,1)} %v_ref.1, bf16[1,256]{1,0:T(2,128)(2,1)} %r_ref.1, f32[8,256]{1,0:T(8,128)} %gi_ref.1, f32[8,256]{1,0:T(8,128)} %ui_ref.1, ...), custom_call_target="tpu_custom_call" | custom-call | flops 10000000000 | bytes 10000000 | tf_op jit(solution)/shard_map/pallas_call | solution.py:352
  134.3 0.6 fusion
  134.9 0.7 copy.12

commit v7 on v6

--- a/solution.py
+++ b/solution.py
@@ -58,7 +58,7 @@
     groups, rows_y, rows_x,
     q_ref, k_ref, v_ref, r_ref, gi_ref, ui_ref, di_ref,
     oq_ref, rows_ref,
-    qbuf, vbuf, rates, ke, kbuf, sbuf, rbuf, gbuf, wg, state, wlow, osl, win, oin,
+    qbuf, vbuf, rates, ke, kbuf, sbuf, rbuf, gbuf, own, wg, state, wlow, osl, win, oin,
     load, feed_s, feed_r, rs_s, rs_r, ag_s, ag_r, fw_s, fw_r, in_s, in_r, if_s, if_r, w_s, w_r, o_s, o_r,
 ):
     chips = rows_y * rows_x
@@ -72,7 +72,7 @@
     hid = state.shape[1]
     half = hid // 2
     per = width * half // 128 // chips
-    share = wg.shape[2]
+    share = own.shape[1]
 
     def ring(d, n):
         return min(d, n - d)
@@ -134,7 +134,7 @@
         for z in range(1, groups):
             pl.semaphore_signal(barrier, inc=1, device_id=(z, tok), device_id_type=MESH)
         firsts = [
-            pltpu.make_async_copy(ref, wg.at[tok, m], load.at[4 + m])
+            pltpu.make_async_copy(ref, own.at[m], load.at[4 + m])
             for m, ref in enumerate((gi_ref, ui_ref, di_ref))
         ]
         for c in firsts:
@@ -146,36 +146,47 @@
         pl.semaphore_signal(barrier, inc=1, device_id=(0, sib), device_id_type=MESH)
         for c in firsts:
             c.wait()
+        for w, value in enumerate(split(own[...].reshape(3 * share, hid))):
+            wg[tok, w] = value
         pl.semaphore_wait(barrier, count + 1)
 
-        def first_copy(n):
-            return copy(wg.at[tok], wg.at[tok], in_s.at[n], in_r.at[n], (0, ahead(n) * 2 + core))
-
-        def first_pass(n):
-            slot = tok if n == count else behind(n) * 2 + core
-            return copy(wg.at[slot], wg.at[slot], if_s.at[n], if_r.at[n], (0, sib))
+        def first_copy(w, n):
+            slot = wg.at[tok, w]
+            return copy(slot, slot, in_s.at[w, n], in_r.at[w, n], (0, ahead(n) * 2 + core))
+
+        def first_pass(w, n):
+            slot = wg.at[tok if n == count else behind(n) * 2 + core, w]
+            return copy(slot, slot, if_s.at[w, n], if_r.at[w, n], (0, sib))
+
+        def first_parts(w):
+            wide = wg[:, w].astype(f32)
+            gate, up, down = (
+                wide[:, m * share : (m + 1) * share].reshape(width, hid) for m in range(3)
+            )
+            return gate.T, up.T, down
+
+        def first_sent(w):
+            for n in range(count):
+                first_copy(w, n).wait_send()
+            for n in range(count + 1):
+                first_pass(w, n).wait_send()
 
         for n in range(count):
-            first_copy(n).start()
-        first_pass(count).start()
+            first_copy(0, n).start()
+        first_pass(0, count).start()
         scale_values()
         kbuf[0, core] = ke[...]
         feed = copy(ke, kbuf.at[0, core], feed_s, feed_r.at[0, core], (0, sib))
         feed.start()
         loads[3].wait()
         for n in reversed(range(count)):
-            first_copy(n).wait_recv()
-            first_pass(n).start()
+            first_copy(0, n).wait_recv()
+            first_pass(0, n).start()
         for n in reversed(range(count + 1)):
-            first_pass(n).wait_recv()
-        state[0] = wg[:, 0].reshape(width, hid).T
-        state[1] = wg[:, 1].reshape(width, hid).T
-        state[2] = wg[:, 2].reshape(hid, width)
+            first_pass(0, n).wait_recv()
+        for m, value in enumerate(first_parts(0)):
+            state[m] = value
         wlow[...] = state[...].astype(bf16)
-        for n in range(count):
-            first_copy(n).wait_send()
-        for n in range(count + 1):
-            first_pass(n).wait_send()
         feed.wait_send()
 
         def pick_outgoing():
@@ -242,7 +253,11 @@
 
             @pl.when(i == 0)
             def _():
+                for n in range(count):
+                    first_copy(1, n).start()
+                first_pass(1, count).start()
                 query([wlow[m] for m in range(3)])
+                first_sent(0)
 
             @pl.when(i > 0)
             def _():
@@ -285,6 +300,12 @@
             def _():
                 pass_feed.wait_recv()
                 pass_feed.start()
+
+            @pl.when(i == 0)
+            def _():
+                for n in reversed(range(count)):
+                    first_copy(1, n).wait_recv()
+                    first_pass(1, n).start()
 
             grads = []
             for m in range(3):
@@ -314,6 +335,14 @@
             @pl.when(i > 1)
             def _():
                 slices_out.wait_send()
+
+            @pl.when(i == 0)
+            def _():
+                for n in reversed(range(count + 1)):
+                    first_pass(1, n).wait_recv()
+                for m, value in enumerate(first_parts(1)):
+                    state[m] = state[m] + value
+                first_sent(1)
 
             for m in range(3):
                 before = state[m]
@@ -366,7 +395,8 @@
                 pltpu.VMEM((chips, 3, per, 128), bf16),
                 pltpu.VMEM((count, 3, per, 128), bf16),
                 pltpu.VMEM((2, 2, chips, 3, per, 128), bf16),
-                pltpu.VMEM((devices, 3, share, hid), f32),
+                pltpu.VMEM((3, share, hid), f32),
+                pltpu.VMEM((devices, 2, 3 * share, hid), bf16),
                 pltpu.VMEM((3, hid, width), f32),
                 pltpu.VMEM((3, hid, width), bf16),
                 pltpu.VMEM((3, share, hid), f32),
@@ -381,10 +411,10 @@
                 dma((count,)),
                 dma((chips,)),
                 dma((2, chips)),
-                dma((count,)),
-                dma((count,)),
-                dma((chips,)),
-                dma((chips,)),
+                dma((2, count)),
+                dma((2, count)),
+                dma((2, chips)),
+                dma((2, chips)),
                 dma,
                 dma,
                 dma,

time: 136 us -> 135 us (level)
  no operation moved by 1% of the time
where the time goes in v7:
time: 135 us
  Pallas kernels  133 us (99%)
    pallas_call x1, Pallas kernels, body(): pl.pallas_call(functools.partial(kernel, groups, rows_y, rows_x), out_sha...  133 us

profile of v7, /device:TPU:1, one launch (start us, length us, event | category | flops | bytes accessed | tf_op | source)
XLA Modules:
  0.0 134.6 jit_solution(10857649200227524723)
XLA Ops:
  0.6 132.7 %shard_map.102 = (bf16[1,256,256]{2,1,0:T(8,128)(2,1)S(1)}, f32[3,8,256]{2,1,0:T(8,128)S(1)}) custom-call(bf16[1,256,256]{2,1,0:T(8,128)(2,1)} %q_ref.1, bf16[1,256,256]{2,1,0:T(8,128)(2,1)} %k_ref.1, bf16[1,256,256]{2,1,0:T(8,128)(2,1)} %v_ref.1, bf16[1,256]{1,0:T(2,128)(2,1)} %r_ref.1, f32[8,256]{1,0:T(8,128)} %gi_ref.1, f32[8,256]{1,0:T(8,128)} %ui_ref.1, ...), custom_call_target="tpu_custom_call" | custom-call | flops 10000000000 | bytes 10000000 | tf_op jit(solution)/shard_map/pallas_call | solution.py:381
  133.3 0.6 fusion
  134.0 0.7 copy.12

commit v8 on v7

--- a/solution.py
+++ b/solution.py
@@ -78,7 +78,7 @@
         return min(d, n - d)
 
     offsets = [(dy, dx) for dy in range(rows_y) for dx in range(rows_x) if (dy, dx) != (0, 0)]
-    offsets.sort(key=lambda o: -(ring(o[0], rows_y) + ring(o[1], rows_x)))
+    offsets.sort(key=lambda o: (-(ring(o[0], rows_y) + ring(o[1], rows_x)), o[1] == 3, o[0] == 3, o[1]))
     count = len(offsets)
 
     def ahead(n):

time: 135 us -> 134 us (level)
  no operation moved by 1% of the time
where the time goes in v8:
time: 134 us; the launch traced here: 133 us
  Pallas kernels  132 us (99%)
    pallas_call x1, Pallas kernels, body(): pl.pallas_call(functools.partial(kernel, groups, rows_y, rows_x), out_sha...  132 us

profile of v8, /device:TPU:1, one launch (start us, length us, event | category | flops | bytes accessed | tf_op | source)
XLA Modules:
  0.0 133.5 jit_solution(8362897929657341160)
XLA Ops:
  0.6 131.6 %shard_map.102 = (bf16[1,256,256]{2,1,0:T(8,128)(2,1)S(1)}, f32[3,8,256]{2,1,0:T(8,128)S(1)}) custom-call(bf16[1,256,256]{2,1,0:T(8,128)(2,1)} %q_ref.1, bf16[1,256,256]{2,1,0:T(8,128)(2,1)} %k_ref.1, bf16[1,256,256]{2,1,0:T(8,128)(2,1)} %v_ref.1, bf16[1,256]{1,0:T(2,128)(2,1)} %r_ref.1, f32[8,256]{1,0:T(8,128)} %gi_ref.1, f32[8,256]{1,0:T(8,128)} %ui_ref.1, ...), custom_call_target="tpu_custom_call" | custom-call | flops 10000000000 | bytes 10000000 | tf_op jit(solution)/shard_map/pallas_call | solution.py:381
  132.2 0.6 fusion
  132.8 0.7 copy.12
